TPU v7x, 32 devices: a whole 2x2x4 slice. The times are simulated.
32 devices in a mesh: parts: 2 (over x), wide: 16 (over z, y, core).
Axes of the slice: x: 2, y: 2, z: 4, core: 2. Of those that a mesh axis runs over, the one named last changes fastest.
Arguments:
- voxels: bfloat16 [32768, 256], P(('parts', 'wide')), parts along dimension 0, may hold values from -16 to 16
- regular_window: int32 [32768], P(('parts', 'wide')), parts along dimension 0, may hold values from 0 to 127, never falling along the last dimension, each value on 1 to 256 neighbouring positions
- shifted_window: int32 [32768], P(('parts', 'wide')), parts along dimension 0, may hold values from 0 to 127, never falling along the last dimension, each value on 1 to 256 neighbouring positions
- dest: int32 [32768], P(('parts', 'wide')), parts along dimension 0, may hold values from 0 to 16383, as said below
- w_qkv: bfloat16 [2, 256, 768], replicated, may hold values from -0.375 to 0.375
- w_out: bfloat16 [2, 256, 256], replicated, may hold values from -1.5 to 1.5
- gain: float32 [2, 256], replicated, may hold values from 0.1 to 1.9
- temper: float32 [2, 8], replicated, may hold values from 0.5 to 6
Outputs:
- shifted_out: bfloat16 [32768, 256], P(('parts', 'wide')), parts along dimension 0
There are 2 independent parts, one for each index of `parts`. A program takes and returns all parts, laid end to end along the dimension named above; an argument that names none is the same for every part. Nothing has to cross between parts.
Inputs may be any that keep to these rules, and one draw needn't show every extreme that they name: `regular_window`: window ids never fall along the order; every window has 1 to 256 voxels and one has exactly 256. `shifted_window`: window ids never fall along the order; every window has 1 to 256 voxels and one has exactly 256. dest is a permutation. Counting blocks of 1024 consecutive positions, at most 128 voxels go from one block of the regular order to one block of the shifted order, and some pair reaches 128; the count from a block to the block k places further along, cyclically, is the same for every block.
All inputs are finite; a program needn't handle non-finite values.
Results may differ from a plain program's by a relative error of at most 0.007.
The roundings to bfloat16 on the way count: a program that leaves them out, or rounds other values in their place, can miss the bound.
Values may be sent and summed in bfloat16 or wider, within the bound.
A program may use at most 64 MiB of HBM per device.

v0:
```python
import math
import jax
import jax.numpy as jnp
from jax import lax
from jax.sharding import PartitionSpec as P

HEADS = 8
epsilon = 1e-05
masked_score = -1e30


def extended(block, sides, width):
    for axis, dim in sides:
        count = lax.axis_size(axis)
        forward = [(i, i + 1) for i in range(count - 1)]
        backward = [(target, source) for source, target in forward]
        low = lax.ppermute(
            lax.slice_in_dim(block, block.shape[dim] - width, None, axis=dim), axis, forward
        )
        high = lax.ppermute(lax.slice_in_dim(block, 0, width, axis=dim), axis, backward)
        block = jnp.concatenate([low, block, high], axis=dim)
    return block


def settle(hidden, attended, w_out_layer, gain_layer):
    summed = hidden.astype(jnp.float32) + jnp.dot(
        attended, w_out_layer, preferred_element_type=jnp.float32
    )
    center = jnp.mean(summed, axis=1, keepdims=True)
    spread = jnp.mean(jnp.square(summed - center), axis=1, keepdims=True)
    return ((summed - center) * lax.rsqrt(spread + epsilon) * gain_layer).astype(jnp.bfloat16)


def window_attention(queries, padded, marks_own, marks_pad, factor, rim_width):
    total_rows = queries.shape[0]
    channels = queries.shape[1]
    head_dim = channels // HEADS
    block_rows = min(512, total_rows)
    key_rows = block_rows + 2 * rim_width
    results = []
    for number in range(total_rows // block_rows):
        first_row = number * block_rows
        query_block = queries[first_row : first_row + block_rows]
        key_block = padded[first_row : first_row + key_rows]
        mark_query = marks_own[first_row : first_row + block_rows]
        mark_key = marks_pad[first_row : first_row + key_rows]
        same_window = mark_query[:, None] == mark_key[None, :]

        def per_head(
            head_index, query_block=query_block, key_block=key_block, same_window=same_window
        ):
            query_part = lax.dynamic_slice_in_dim(query_block, head_index * head_dim, head_dim, 1)
            keys_part = lax.dynamic_slice_in_dim(key_block, head_index * head_dim, head_dim, 1)
            values_part = lax.dynamic_slice_in_dim(
                key_block, channels + head_index * head_dim, head_dim, 1
            )
            scores = lax.dot_general(
                query_part, keys_part, (((1,), (1,)), ((), ())), preferred_element_type=jnp.float32
            )
            scores = scores * factor[head_index]
            scores = jnp.where(same_window, scores, masked_score)
            highest = jnp.max(scores, axis=1, keepdims=True)
            exponents = jnp.where(same_window, jnp.exp(scores - highest), 0.0)
            totals = jnp.sum(exponents, axis=1, keepdims=True)
            weights = (exponents / totals).astype(jnp.bfloat16)
            return jnp.dot(weights, values_part, preferred_element_type=jnp.float32).astype(
                jnp.bfloat16
            )

        heads_out = lax.map(per_head, jnp.arange(HEADS, dtype=jnp.int32))
        results.append(jnp.transpose(heads_out, (1, 0, 2)).reshape(block_rows, channels))
    return jnp.concatenate(results, axis=0)


def sublayer(hidden, window_ids, w_qkv_layer, w_out_layer, gain_layer, temper_layer):
    local_rows = hidden.shape[0]
    channels = hidden.shape[1]
    rim_width = local_rows // 4
    marks = window_ids + 1
    factor = temper_layer * (1.0 / math.sqrt(channels // HEADS))
    projected = jnp.dot(hidden, w_qkv_layer, preferred_element_type=jnp.float32).astype(
        jnp.bfloat16
    )
    key_vals = projected[:, channels:]
    padded, marks_pad = (
        extended(key_vals, (("wide", 0),), rim_width),
        extended(marks, (("wide", 0),), rim_width),
    )
    queries = projected[:, :channels]
    attended = window_attention(queries, padded, marks, marks_pad, factor, rim_width)
    return settle(hidden, attended, w_out_layer, gain_layer)


def regroup_rows(first, dest):
    local_rows = first.shape[0]
    channels = first.shape[1]
    devices = lax.axis_size("wide")
    capacity = 2 * local_rows // devices
    target = dest // local_rows
    slot_within = dest - target * local_rows
    matches = (target[:, None] == jnp.arange(devices, dtype=jnp.int32)[None, :]).astype(jnp.int32)
    position = jnp.sum(jnp.cumsum(matches, axis=0) * matches, axis=1) - 1
    buffer_row = target * capacity + position
    outgoing = jnp.zeros((devices * capacity, channels), jnp.bfloat16).at[buffer_row].set(first)
    slot_list = (
        jnp.full((devices * capacity,), local_rows, jnp.int32).at[buffer_row].set(slot_within)
    )
    arrived, arrived_slots = (
        lax.all_to_all(outgoing, "wide", split_axis=0, concat_axis=0, tiled=True),
        lax.all_to_all(slot_list, "wide", split_axis=0, concat_axis=0, tiled=True),
    )
    return (
        jnp.zeros((local_rows, channels), jnp.bfloat16).at[arrived_slots].set(arrived, mode="drop")
    )


def body(voxels, regular_window, shifted_window, dest, w_qkv, w_out, gain, temper):
    first = sublayer(voxels, regular_window, w_qkv[0], w_out[0], gain[0], temper[0])
    moved = regroup_rows(first, dest)
    return sublayer(moved, shifted_window, w_qkv[1], w_out[1], gain[1], temper[1])


def solution(mesh):
    in_specs = (
        P(("parts", "wide"), None),
        P(("parts", "wide")),
        P(("parts", "wide")),
        P(("parts", "wide")),
        P(),
        P(),
        P(),
        P(),
    )
    out_specs = P(("parts", "wide"), None)
    return jax.shard_map(body, mesh=mesh, in_specs=in_specs, out_specs=out_specs, check_vma=False)
```

profile of v0, /device:TPU:13, one launch (start us, length us, event | category | flops | bytes accessed | tf_op | source)
XLA Modules:
  0.0 406.4 jit_solution(13931724288074019573)
XLA Ops:
  2.6 3.8 collective-permute-start
  8.4 4.5 %collective-permute-start.1 = (s32[256]{0:T(256)S(1)}, s32[256]{0:T(256)S(1)}, u32[]{:S(2)}, u32[]{:S(2)}) collective-permute-start(s32[256]{0:T(256)S(1)} %get-tuple-element.539), channel_id=1, source_target_pairs={{0,1},{1,2},{2,3},{3,4},{4,5},{5,6},{6,7},{7,8},{8,9},{9,10},{10,1... | collective-permute-start | bytes 3080 | tf_op jit(solution)/shard_map/ppermute | solution.py:17
  14.9 4.5 %reduce-window.6 = s32[16,8,128]{2,1,0:T(8,128)S(1)} reduce-window(s32[16,8,128]{2,1,0:T(8,128)S(1)} %fusion.76, s32[]{:T(128)} %constant.259.clone.1), window={size=1x1x128 pad=0_0x0_0x127_0}, to_apply=%region_0.1 | reduce-window | flops 2080768 | bytes 131076 | tf_op jit(solution)/shard_map/reduce-window
  19.9 4.9 %scatter_custom_fusion = s32[2048]{0:T(1024)} fusion(s32[1024]{0:T(1024)S(1)} %get-tuple-element.542, s32[1024]{0:T(1024)S(1)} %get-tuple-element.541, s32[]{:T(128)} %constant.257.clone.1), kind=kCustom, calls=%fused_computation.123 | custom fusion | bytes 8196 | tf_op jit(solution)/shard_map/scatter | solution.py:106
  24.8 6.4 %all-to-all-start = ((s32[16,128,1]{1,2,0:T(1,128)}), s32[16,128,1]{1,2,0:T(1,128)S(1)}, u32[]{:S(2)}, u32[]{:S(2)}) async-start(s32[16,128,1]{1,2,0:T(1,128)} %bitcast.4), calls=%async_computation | async-start | bytes 16384 | tf_op jit(solution)/shard_map/all_to_all | solution.py:110
  35.7 78.1 %while.52 = (s32[]{:T(128)}, bf16[8,512,32]{1,2,0:T(8,128)(2,1)S(1)}, s32[8]{0:T(128)S(1)}, bf16[512,256]{1,0:T(8,128)(2,1)}, bf16[1024,512]{1,0:T(8,128)(2,1)},...) while((s32[]{:T(128)}, ...), condition=%wide.region_7.8_spmd.clone, body=%wide.region_4.7_spmd.clone.sunk | while | flops 76037128 | bytes 7010112 | solution.py:70
  43.0 2.5 fusion.116
  52.7 2.5 fusion.116
  62.5 2.5 fusion.116
  72.2 2.5 fusion.116
  82.0 2.5 fusion.116
  91.8 2.5 fusion.116
  101.5 2.5 fusion.116
  111.3 2.5 fusion.116
  113.9 74.5 %while.53 = (s32[]{:T(128)}, bf16[8,512,32]{1,2,0:T(8,128)(2,1)S(1)}, s32[8]{0:T(128)S(1)}, bf16[512,256]{1,0:T(8,128)(2,1)}, bf16[1024,512]{1,0:T(8,128)(2,1)},...) while((s32[]{:T(128)}, ...), condition=%wide.region_11.12_spmd.clone, body=%wide.region_8.11_spmd.clone.sunk | while | flops 76037128 | bytes 7010112 | solution.py:70
  189.3 6.0 %scatter_custom_fusion.1 = bf16[2048,256]{1,0:T(8,128)(2,1)} fusion(s32[1024]{0:T(1024)S(1)} %get-tuple-element.542, bf16[1024,256]{1,0:T(8,128)(2,1)S(1)} %copy.23, bf16[]{:T(256)} %constant.256.clone.1), kind=kCustom, calls=%fused_computation.89 | custom fusion | bytes 1048578 | tf_op jit(solution)/shard_map/scatter | solution.py:104
  195.3 6.0 %all-to-all-start.1 = ((bf16[16,128,256]{2,1,0:T(8,128)(2,1)}), bf16[16,128,256]{2,1,0:T(8,128)(2,1)S(1)}, u32[]{:S(2)}, u32[]{:S(2)}) async-start(bf16[16,128,256]{2,1,0:T(8,128)(2,1)} %bitcast.15), calls=%async_computation.1 | async-start | bytes 2097152 | tf_op jit(solution)/shard_map/all_to_all | solution.py:109
  201.4 3.4 collective-permute-start.5
  206.9 19.3 %all-to-all-done.1 = bf16[16,128,256]{2,1,0:T(8,128)(2,1)S(1)} async-done(((bf16[16,128,256]{2,1,0:T(8,128)(2,1)}), bf16[16,128,256]{2,1,0:T(8,128)(2,1)S(1)}, u32[]{:S(2)}, u32[]{:S(2)}) %all-to-all-start.1) | async-done | bytes 1048608 | tf_op jit(solution)/shard_map/all_to_all | solution.py:109
  226.2 9.4 %scatter_custom_fusion.2 = bf16[1024,256]{1,0:T(8,128)(2,1)S(1)} fusion(s32[2048]{0:T(1024)S(1)} %bitcast.115, bf16[2048,256]{1,0:T(8,128)(2,1)S(1)} %bitcast.112, bf16[]{:T(256)} %constant.256.clone.1), kind=kCustom, calls=%fused_computation.95 | custom fusion | bytes 524290 | tf_op jit(solution)/shard_map/scatter | solution.py:113
  237.0 3.7 collective-permute-start.4
  244.5 5.0 %collective-permute-done.6 = bf16[256,512]{1,0:T(8,128)(2,1)} collective-permute-done((bf16[256,512]{1,0:T(8,128)(2,1)}, bf16[256,512]{1,0:T(8,128)(2,1)}, u32[]{:S(2)}, u32[]{:S(2)}) %collective-permute-start.6) | collective-permute-done | bytes 262176 | tf_op jit(solution)/shard_map/ppermute | solution.py:20
  252.1 78.1 %while.54 = (s32[]{:T(128)}, bf16[8,512,32]{1,2,0:T(8,128)(2,1)S(1)}, s32[8]{0:T(128)S(1)}, bf16[512,256]{1,0:T(8,128)(2,1)}, bf16[1024,512]{1,0:T(8,128)(2,1)},...) while((s32[]{:T(128)}, ...), condition=%wide.region_19.20_spmd.clone, body=%wide.region_16.19_spmd.clone.sunk | while | flops 76037128 | bytes 7010112 | solution.py:70
  259.3 2.5 fusion.124
  269.1 2.5 fusion.124
  278.8 2.5 fusion.124
  288.6 2.5 fusion.124
  298.3 2.5 fusion.124
  308.1 2.5 fusion.124
  317.9 2.5 fusion.124
  327.6 2.5 fusion.124
  330.2 74.5 %while.55 = (s32[]{:T(128)}, bf16[8,512,32]{1,2,0:T(8,128)(2,1)S(1)}, s32[8]{0:T(128)S(1)}, bf16[512,256]{1,0:T(8,128)(2,1)}, bf16[1024,512]{1,0:T(8,128)(2,1)},...) while((s32[]{:T(128)}, ...), condition=%wide.region_23.24_spmd.clone, body=%wide.region_20.23_spmd.clone.sunk | while | flops 76037128 | bytes 7010112 | solution.py:70
  (231 shorter events, 212.1 us)
Async XLA Ops:
  0.0 8.4 %copy-start.7 = (s32[1024]{0:T(1024)S(1)}, s32[1024]{0:T(1024)}, u32[]{:S(2)}) copy-start(s32[1024]{0:T(1024)} %param.17) | copy-start | bytes 12292
  0.0 14.9 %copy-start.6 = (s32[1024]{0:T(1024)S(1)}, s32[1024]{0:T(1024)}, u32[]{:S(2)}) copy-start(s32[1024]{0:T(1024)} %param.19) | copy-start | bytes 12292
  0.0 32.0 %copy-start.9 = (f32[2,256]{1,0:T(2,128)S(1)}, f32[2,256]{1,0:T(2,128)}, u32[]{:S(2)}) copy-start(f32[2,256]{1,0:T(2,128)} %param.22) | copy-start | bytes 6148
  0.0 32.0 %copy-start.10 = (f32[2,8]{1,0:T(2,128)S(1)}, f32[2,8]{1,0:T(2,128)}, u32[]{:S(2)}) copy-start(f32[2,8]{1,0:T(2,128)} %param.23) | copy-start | bytes 196
  2.6 29.5 %copy-start = (bf16[1024,256]{1,0:T(8,128)(2,1)S(1)}, bf16[1024,256]{1,0:T(8,128)(2,1)}, u32[]{:S(2)}) copy-start(bf16[1024,256]{1,0:T(8,128)(2,1)} %param.16) | copy-start | bytes 1572868
  2.6 30.6 %collective-permute-start = (bf16[256,512]{1,0:T(8,128)(2,1)}, bf16[256,512]{1,0:T(8,128)(2,1)S(1)}, u32[]{:S(2)}, u32[]{:S(2)}) collective-permute-start(bf16[256,512]{1,0:T(8,128)(2,1)} %get-tuple-element.521), channel_id=1, source_target_pairs={{0,1},{1,2},{2,3},{3,4},{4,5},{5,6},{6,7},{7,8},{8,9},{9,10},{10,1... | collective-permute-start | bytes 786440 | tf_op jit(solution)/shard_map/ppermute | solution.py:17
  6.5 26.7 %collective-permute-start.2 = (bf16[256,512]{1,0:T(8,128)(2,1)}, bf16[256,512]{1,0:T(8,128)(2,1)}, u32[]{:S(2)}, u32[]{:S(2)}) collective-permute-start(bf16[256,512]{1,0:T(8,128)(2,1)} %get-tuple-element.522), channel_id=1, source_target_pairs={{1,0},{2,1},{3,2},{4,3},{5,4},{6,5},{7,6},{8,7},{9,8},{10,9},{11,1... | collective-permute-start | bytes 786440 | tf_op jit(solution)/shard_map/ppermute | solution.py:20
  8.4 24.8 %collective-permute-start.1 = (s32[256]{0:T(256)S(1)}, s32[256]{0:T(256)S(1)}, u32[]{:S(2)}, u32[]{:S(2)}) collective-permute-start(s32[256]{0:T(256)S(1)} %get-tuple-element.539), channel_id=1, source_target_pairs={{0,1},{1,2},{2,3},{3,4},{4,5},{5,6},{6,7},{7,8},{8,9},{9,10},{10,1... | collective-permute-start | bytes 3080 | tf_op jit(solution)/shard_map/ppermute | solution.py:17
  13.0 20.2 %collective-permute-start.3 = (s32[256]{0:T(256)S(1)}, s32[256]{0:T(256)S(1)}, u32[]{:S(2)}, u32[]{:S(2)}) collective-permute-start(s32[256]{0:T(256)S(1)} %get-tuple-element.540), channel_id=1, source_target_pairs={{1,0},{2,1},{3,2},{4,3},{5,4},{6,5},{7,6},{8,7},{9,8},{10,9},{11,1... | collective-permute-start | bytes 3080 | tf_op jit(solution)/shard_map/ppermute | solution.py:20
  24.8 170.5 %all-to-all-start = ((s32[16,128,1]{1,2,0:T(1,128)}), s32[16,128,1]{1,2,0:T(1,128)S(1)}, u32[]{:S(2)}, u32[]{:S(2)}) async-start(s32[16,128,1]{1,2,0:T(1,128)} %bitcast.4), calls=%async_computation | async-start | bytes 16384 | tf_op jit(solution)/shard_map/all_to_all | solution.py:110
  113.8 74.5 %copy-start.1 = (bf16[1024,256]{0,1:T(8,128)(2,1)S(1)}, bf16[1024,256]{0,1:T(8,128)(2,1)}, u32[]{:S(2)}) copy-start(bf16[1024,256]{0,1:T(8,128)(2,1)} %copy.22) | copy-start | bytes 1572868
  113.9 74.5 %copy-start.4 = (bf16[2,256,256]{2,1,0:T(8,128)(2,1)S(1)}, bf16[2,256,256]{2,1,0:T(8,128)(2,1)}, u32[]{:S(2)}) copy-start(bf16[2,256,256]{2,1,0:T(8,128)(2,1)} %param.21) | copy-start | bytes 786436
  189.1 12.3 %copy-start.8 = (s32[1024]{0:T(1024)S(1)}, s32[1024]{0:T(1024)}, u32[]{:S(2)}) copy-start(s32[1024]{0:T(1024)} %param.18) | copy-start | bytes 12292
  189.3 46.3 %copy-start.3 = (bf16[2,256,768]{2,1,0:T(8,128)(2,1)S(1)}, bf16[2,256,768]{2,1,0:T(8,128)(2,1)}, u32[]{:S(2)}) copy-start(bf16[2,256,768]{2,1,0:T(8,128)(2,1)} %param.20) | copy-start | bytes 2359300
  195.3 30.9 %all-to-all-start.1 = ((bf16[16,128,256]{2,1,0:T(8,128)(2,1)}), bf16[16,128,256]{2,1,0:T(8,128)(2,1)S(1)}, u32[]{:S(2)}, u32[]{:S(2)}) async-start(bf16[16,128,256]{2,1,0:T(8,128)(2,1)} %bitcast.15), calls=%async_computation.1 | async-start | bytes 2097152 | tf_op jit(solution)/shard_map/all_to_all | solution.py:109
  201.4 41.2 %collective-permute-start.5 = (s32[256]{0:T(256)S(1)}, s32[256]{0:T(256)S(1)}, u32[]{:S(2)}, u32[]{:S(2)}) collective-permute-start(s32[256]{0:T(256)S(1)} %get-tuple-element.533), channel_id=1, source_target_pairs={{0,1},{1,2},{2,3},{3,4},{4,5},{5,6},{6,7},{7,8},{8,9},{9,10},{10,1... | collective-permute-start | bytes 3080 | tf_op jit(solution)/shard_map/ppermute | solution.py:17
  204.8 37.8 %collective-permute-start.7 = (s32[256]{0:T(256)S(1)}, s32[256]{0:T(256)S(1)}, u32[]{:S(2)}, u32[]{:S(2)}) collective-permute-start(s32[256]{0:T(256)S(1)} %get-tuple-element.534), channel_id=1, source_target_pairs={{1,0},{2,1},{3,2},{4,3},{5,4},{6,5},{7,6},{8,7},{9,8},{10,9},{11,1... | collective-permute-start | bytes 3080 | tf_op jit(solution)/shard_map/ppermute | solution.py:20
  237.0 7.6 %collective-permute-start.4 = (bf16[256,512]{1,0:T(8,128)(2,1)}, bf16[256,512]{1,0:T(8,128)(2,1)S(1)}, u32[]{:S(2)}, u32[]{:S(2)}) collective-permute-start(bf16[256,512]{1,0:T(8,128)(2,1)} %get-tuple-element.517), channel_id=1, source_target_pairs={{0,1},{1,2},{2,3},{3,4},{4,5},{5,6},{6,7},{7,8},{8,9},{9,10},{10,1... | collective-permute-start | bytes 786440 | tf_op jit(solution)/shard_map/ppermute | solution.py:17
  240.6 8.9 %collective-permute-start.6 = (bf16[256,512]{1,0:T(8,128)(2,1)}, bf16[256,512]{1,0:T(8,128)(2,1)}, u32[]{:S(2)}, u32[]{:S(2)}) collective-permute-start(bf16[256,512]{1,0:T(8,128)(2,1)} %get-tuple-element.518), channel_id=1, source_target_pairs={{1,0},{2,1},{3,2},{4,3},{5,4},{6,5},{7,6},{8,7},{9,8},{10,9},{11,1... | collective-permute-start | bytes 786440 | tf_op jit(solution)/shard_map/ppermute | solution.py:20
  330.2 74.5 %copy-start.2 = (bf16[1024,256]{0,1:T(8,128)(2,1)S(1)}, bf16[1024,256]{0,1:T(8,128)(2,1)}, u32[]{:S(2)}) copy-start(bf16[1024,256]{0,1:T(8,128)(2,1)} %copy.24) | copy-start | bytes 1572868
  330.2 74.5 %copy-start.5 = (bf16[2,256,256]{2,1,0:T(8,128)(2,1)S(1)}, bf16[2,256,256]{2,1,0:T(8,128)(2,1)}, u32[]{:S(2)}) copy-start(bf16[2,256,256]{2,1,0:T(8,128)(2,1)} %param.21) | copy-start | bytes 786436
where the time goes:
time: 410 us; the launch traced here: 406 us
  matrix products  153 us (37%)
  loops' own time  76.8 us (19%)
  local copies, waits for them, and re-layouts  65 us (16%)
  other arithmetic  50.9 us (12%)
  starting transfers between devices  35.7 us (9%)
  waiting for transfers between devices  24.3 us (6%)
    dot_general x32, matrix products, per_head(): jnp.dot(weights, values_part, preferred_element_type=jnp.float32)  79.2 us
    another operation x4, loops' own time, window_attention(): heads_out = lax.map(per_head, jnp.arange(HEADS, dtype=jnp.int32))  76.8 us
    dot_general x32, matrix products, per_head(): lax.dot_general(query_part, keys_part, (((1,), (1,)), ((), ())), preferre...  71 us
    reduce_sum x32, other arithmetic, per_head(): totals = jnp.sum(exponents, axis=1, keepdims=True)  40.6 us
    all_to_all x1, waiting for transfers between devices, regroup_rows(): lax.all_to_all(outgoing, 'wide', split_axis=0, concat_axis=0, tiled=True)  19.3 us
    dynamic_slice x32, local copies, waits for them, and re-layouts, window_attention(): heads_out = lax.map(per_head, jnp.arange(HEADS, dtype=jnp.int32))  18.8 us
    dynamic_slice x32, local copies, waits for them, and re-layouts, per_head(): scores = scores * factor[head_index]  18.8 us
    ppermute x4, starting transfers between devices, extended(): lax.ppermute(lax.slice_in_dim(block, block.shape[dim] - width, None, axis...  15.4 us
  transfers between devices with their start and end apart: 10, of which 2 were waited for; matrix products, arithmetic and copies ran while one was open for 36% of the time, Pallas kernels for 0%

commit v1 on v0

--- a/solution.py
+++ b/solution.py
@@ -7,6 +7,22 @@
 HEADS = 8
 epsilon = 1e-05
 masked_score = -1e30
+
+
+def pairwise_exchange(x, axis, split, join):
+    ways, here = (lax.axis_size(axis), lax.axis_index(axis))
+    width = x.shape[split] // ways
+    dims = list(x.shape)
+    dims[split] = width
+    height = dims[join]
+    dims[join] = height * ways
+    full = jnp.zeros(dims, x.dtype)
+    for mask in range(ways):
+        part = lax.dynamic_slice_in_dim(x, (here ^ mask) * width, width, axis=split)
+        if mask:
+            part = lax.ppermute(part, axis, [(d, d ^ mask) for d in range(ways)])
+        full = lax.dynamic_update_slice_in_dim(full, part, (here ^ mask) * height, axis=join)
+    return full
 
 
 def extended(block, sides, width):
@@ -106,7 +122,7 @@
         jnp.full((devices * capacity,), local_rows, jnp.int32).at[buffer_row].set(slot_within)
     )
     arrived, arrived_slots = (
-        lax.all_to_all(outgoing, "wide", split_axis=0, concat_axis=0, tiled=True),
+        pairwise_exchange(outgoing, "wide", 0, 0),
         lax.all_to_all(slot_list, "wide", split_axis=0, concat_axis=0, tiled=True),
     )
     return (

time: 410 us -> 431 us (1.051)
  starting transfers between devices: 35.7 us -> 51.2 us
  waiting for transfers between devices: 24.3 us -> 18.3 us
    ppermute x0 -> x15, starting transfers between devices: none -> 21.4 us  [pairwise_exchange(): part = lax.ppermute(part, axis, [(d, d ^ mask) for d in range(ways)])]
    all_to_all x1 -> x0, waiting for transfers between devices: 19.3 us -> none  [regroup_rows(): lax.all_to_all(outgoing, 'wide', split_axis=0, concat_axis=0, tiled=True)]
    ppermute x0 -> x15, waiting for transfers between devices: none -> 14.2 us  [pairwise_exchange(): part = lax.ppermute(part, axis, [(d, d ^ mask) for d in range(ways)])]
    all_to_all x1 -> x0, starting transfers between devices: 6.01 us -> none  [regroup_rows(): lax.all_to_all(outgoing, 'wide', split_axis=0, concat_axis=0, tiled=True)]
  transfers between devices with their start and end apart: 10 -> 24, of which waited for: 2 -> 10; matrix products, arithmetic and copies ran while one was open for 36% -> 36% of each run, Pallas kernels for 0% -> 0%
where the time goes in v1:
time: 431 us; the launch traced here: 426 us
  matrix products  154 us (36%)
  loops' own time  80.9 us (19%)
  local copies, waits for them, and re-layouts  66.2 us (15%)
  other arithmetic  54.3 us (13%)
  starting transfers between devices  51.2 us (12%)
  waiting for transfers between devices  18.3 us (4%)
    another operation x4, loops' own time, window_attention(): heads_out = lax.map(per_head, jnp.arange(HEADS, dtype=jnp.int32))  80.9 us
    dot_general x32, matrix products, per_head(): jnp.dot(weights, values_part, preferred_element_type=jnp.float32)  80.2 us
    dot_general x32, matrix products, per_head(): lax.dot_general(query_part, keys_part, (((1,), (1,)), ((), ())), preferre...  71 us
    reduce_sum x32, other arithmetic, per_head(): totals = jnp.sum(exponents, axis=1, keepdims=True)  41.6 us
    ppermute x15, starting transfers between devices, pairwise_exchange(): part = lax.ppermute(part, axis, [(d, d ^ mask) for d in range(ways)])  21.4 us
    dynamic_slice x32, local copies, waits for them, and re-layouts, window_attention(): heads_out = lax.map(per_head, jnp.arange(HEADS, dtype=jnp.int32))  19 us
    dynamic_slice x32, local copies, waits for them, and re-layouts, per_head(): scores = scores * factor[head_index]  19 us
    ppermute x4, starting transfers between devices, extended(): lax.ppermute(lax.slice_in_dim(block, block.shape[dim] - width, None, axis...  15.7 us
  transfers between devices with their start and end apart: 24, of which 10 were waited for; matrix products, arithmetic and copies ran while one was open for 36% of the time, Pallas kernels for 0%

profile of v1, /device:TPU:13, one launch (start us, length us, event | category | flops | bytes accessed | tf_op | source)
XLA Modules:
  0.0 425.9 jit_solution(10300831866252678732)
XLA Ops:
  2.6 3.8 collective-permute-start
  8.4 4.5 %collective-permute-start.1 = (s32[256]{0:T(256)S(1)}, s32[256]{0:T(256)S(1)}, u32[]{:S(2)}, u32[]{:S(2)}) collective-permute-start(s32[256]{0:T(256)S(1)} %get-tuple-element.555), channel_id=1, source_target_pairs={{0,1},{1,2},{2,3},{3,4},{4,5},{5,6},{6,7},{7,8},{8,9},{9,10},{10,1... | collective-permute-start | bytes 3080 | tf_op jit(solution)/shard_map/ppermute | solution.py:33
  14.9 4.5 %reduce-window.6 = s32[16,8,128]{2,1,0:T(8,128)S(1)} reduce-window(s32[16,8,128]{2,1,0:T(8,128)S(1)} %fusion.78, s32[]{:T(128)} %constant.279.clone.1), window={size=1x1x128 pad=0_0x0_0x127_0}, to_apply=%region_0.1 | reduce-window | flops 2080768 | bytes 131076 | tf_op jit(solution)/shard_map/reduce-window
  19.9 4.9 %scatter_custom_fusion = s32[2048]{0:T(1024)} fusion(s32[1024]{0:T(1024)S(1)} %get-tuple-element.558, s32[1024]{0:T(1024)S(1)} %get-tuple-element.557, s32[]{:T(128)} %constant.277.clone.1), kind=kCustom, calls=%fused_computation.156 | custom fusion | bytes 8196 | tf_op jit(solution)/shard_map/scatter | solution.py:122
  24.8 6.4 %all-to-all-start = ((s32[16,128,1]{1,2,0:T(1,128)}), s32[16,128,1]{1,2,0:T(1,128)}, u32[]{:S(2)}, u32[]{:S(2)}) async-start(s32[16,128,1]{1,2,0:T(1,128)} %bitcast.4), calls=%async_computation | async-start | bytes 16384 | tf_op jit(solution)/shard_map/all_to_all | solution.py:126
  31.8 3.5 collective-permute-start.20
  42.0 79.1 %while.52 = (s32[]{:T(128)}, bf16[8,512,32]{1,2,0:T(8,128)(2,1)S(1)}, s32[8]{0:T(128)S(1)}, bf16[512,256]{1,0:T(8,128)(2,1)S(1)}, bf16[1024,512]{1,0:T(8,128)(2,...) while((s32[]{:T(128)}, ...), condition=%wide.region_7.8_spmd.clone, body=%wide.region_4.7_spmd.clone.sunk | while | flops 76037128 | bytes 7010112 | solution.py:86
  49.4 2.5 fusion.117
  59.2 2.5 fusion.117
  69.1 2.5 fusion.117
  79.0 2.5 fusion.117
  88.9 2.5 fusion.117
  98.8 2.5 fusion.117
  108.7 2.5 fusion.117
  118.6 2.5 fusion.117
  121.2 79.5 %while.53 = (s32[]{:T(128)}, bf16[8,512,32]{1,2,0:T(8,128)(2,1)S(1)}, s32[8]{0:T(128)S(1)}, bf16[512,256]{1,0:T(8,128)(2,1)}, bf16[1024,512]{1,0:T(8,128)(2,1)},...) while((s32[]{:T(128)}, ...), condition=%wide.region_11.12_spmd.clone, body=%wide.region_8.11_spmd.clone.sunk | while | flops 76037128 | bytes 7010112 | solution.py:86
  128.6 2.5 fusion.121
  138.5 2.5 fusion.121
  148.5 2.5 fusion.121
  158.4 2.5 fusion.121
  168.3 2.5 fusion.121
  201.6 5.5 %scatter_custom_fusion.1 = bf16[2048,256]{1,0:T(8,128)(2,1)S(1)} fusion(s32[1024]{0:T(1024)S(1)} %get-tuple-element.558, bf16[1024,256]{1,0:T(8,128)(2,1)S(1)} %copy.23, bf16[]{:T(256)} %constant.276.clone.1), kind=kCustom, calls=%fused_computation.90 | custom fusion | bytes 1048578 | tf_op jit(solution)/shard_map/scatter | solution.py:120
  220.2 2.8 collective-permute-start.12
  224.3 5.2 %collective-permute-start.14 = (bf16[128,256]{1,0:T(8,128)(2,1)S(1)}, bf16[128,256]{1,0:T(8,128)(2,1)S(1)}, u32[]{:S(2)}, u32[]{:S(2)}) collective-permute-start(bf16[128,256]{1,0:T(8,128)(2,1)S(1)} %get-tuple-element.531), channel_id=1, source_target_pairs={{0,11},{1,10},{2,9},{3,8},{4,15},{5,14},{6,13},{7,12},{8,3},{9,2},... | collective-permute-start | bytes 196616 | tf_op jit(solution)/shard_map/ppermute | solution.py:23
  237.0 3.3 collective-permute-done.17
  240.4 4.2 collective-permute-done.18
  244.6 9.4 %scatter_custom_fusion.2 = bf16[1024,256]{1,0:T(8,128)(2,1)S(1)} fusion(s32[2048]{0:T(1024)S(1)} %bitcast.112, bf16[2048,256]{1,0:T(8,128)(2,1)S(1)} %constant_dynamic-update-slice_fusion, bf16[]{:T(256)} %constant.276.clone.1), kind=kCustom, calls=%fused_computation.97 | custom fusion | bytes 524290 | tf_op jit(solution)/shard_map/scatter | solution.py:129
  255.3 3.8 collective-permute-start.19
  263.8 4.2 collective-permute-done.21
  268.0 2.9 pad_maximum_fusion.1
  270.9 74.0 %while.54 = (s32[]{:T(128)}, bf16[8,512,32]{1,2,0:T(8,128)(2,1)S(1)}, s32[8]{0:T(128)S(1)}, bf16[512,256]{1,0:T(8,128)(2,1)S(1)}, bf16[1024,512]{1,0:T(8,128)(2,...) while((s32[]{:T(128)}, ...), condition=%wide.region_19.20_spmd.clone, body=%wide.region_16.19_spmd.clone.sunk | while | flops 76037128 | bytes 7010112 | solution.py:86
  345.0 79.1 %while.55 = (s32[]{:T(128)}, bf16[8,512,32]{1,2,0:T(8,128)(2,1)S(1)}, s32[8]{0:T(128)S(1)}, bf16[512,256]{1,0:T(8,128)(2,1)}, bf16[1024,512]{1,0:T(8,128)(2,1)},...) while((s32[]{:T(128)}, ...), condition=%wide.region_23.24_spmd.clone, body=%wide.region_20.23_spmd.clone.sunk | while | flops 76037128 | bytes 7010112 | solution.py:86
  (282 shorter events, 242.5 us)
Async XLA Ops:
  0.0 8.4 %copy-start.9 = (s32[1024]{0:T(1024)S(1)}, s32[1024]{0:T(1024)}, u32[]{:S(2)}) copy-start(s32[1024]{0:T(1024)} %param.17) | copy-start | bytes 12292
  0.0 14.9 %copy-start.7 = (s32[1024]{0:T(1024)S(1)}, s32[1024]{0:T(1024)}, u32[]{:S(2)}) copy-start(s32[1024]{0:T(1024)} %param.19) | copy-start | bytes 12292
  0.0 31.2 %copy-start.10 = (s32[1024]{0:T(1024)S(1)}, s32[1024]{0:T(1024)}, u32[]{:S(2)}) copy-start(s32[1024]{0:T(1024)} %param.18) | copy-start | bytes 12292
  2.6 33.6 %copy-start = (bf16[1024,256]{1,0:T(8,128)(2,1)S(1)}, bf16[1024,256]{1,0:T(8,128)(2,1)}, u32[]{:S(2)}) copy-start(bf16[1024,256]{1,0:T(8,128)(2,1)} %param.16) | copy-start | bytes 1572868
  2.6 36.9 %collective-permute-start = (bf16[256,512]{1,0:T(8,128)(2,1)}, bf16[256,512]{1,0:T(8,128)(2,1)S(1)}, u32[]{:S(2)}, u32[]{:S(2)}) collective-permute-start(bf16[256,512]{1,0:T(8,128)(2,1)} %get-tuple-element.521), channel_id=1, source_target_pairs={{0,1},{1,2},{2,3},{3,4},{4,5},{5,6},{6,7},{7,8},{8,9},{9,10},{10,1... | collective-permute-start | bytes 786440 | tf_op jit(solution)/shard_map/ppermute | solution.py:33
  6.4 33.1 %collective-permute-start.2 = (bf16[256,512]{1,0:T(8,128)(2,1)}, bf16[256,512]{1,0:T(8,128)(2,1)}, u32[]{:S(2)}, u32[]{:S(2)}) collective-permute-start(bf16[256,512]{1,0:T(8,128)(2,1)} %get-tuple-element.522), channel_id=1, source_target_pairs={{1,0},{2,1},{3,2},{4,3},{5,4},{6,5},{7,6},{8,7},{9,8},{10,9},{11,1... | collective-permute-start | bytes 786440 | tf_op jit(solution)/shard_map/ppermute | solution.py:36
  8.4 29.2 %collective-permute-start.1 = (s32[256]{0:T(256)S(1)}, s32[256]{0:T(256)S(1)}, u32[]{:S(2)}, u32[]{:S(2)}) collective-permute-start(s32[256]{0:T(256)S(1)} %get-tuple-element.555), channel_id=1, source_target_pairs={{0,1},{1,2},{2,3},{3,4},{4,5},{5,6},{6,7},{7,8},{8,9},{9,10},{10,1... | collective-permute-start | bytes 3080 | tf_op jit(solution)/shard_map/ppermute | solution.py:33
  13.0 26.6 %collective-permute-start.3 = (s32[256]{0:T(256)S(1)}, s32[256]{0:T(256)S(1)}, u32[]{:S(2)}, u32[]{:S(2)}) collective-permute-start(s32[256]{0:T(256)S(1)} %get-tuple-element.556), channel_id=1, source_target_pairs={{1,0},{2,1},{3,2},{4,3},{5,4},{6,5},{7,6},{8,7},{9,8},{10,9},{11,1... | collective-permute-start | bytes 3080 | tf_op jit(solution)/shard_map/ppermute | solution.py:36
  24.8 183.9 %all-to-all-start = ((s32[16,128,1]{1,2,0:T(1,128)}), s32[16,128,1]{1,2,0:T(1,128)}, u32[]{:S(2)}, u32[]{:S(2)}) async-start(s32[16,128,1]{1,2,0:T(1,128)} %bitcast.4), calls=%async_computation | async-start | bytes 16384 | tf_op jit(solution)/shard_map/all_to_all | solution.py:126
  31.8 229.3 %collective-permute-start.20 = (s32[256]{0:T(256)}, s32[256]{0:T(256)}, u32[]{:S(2)}, u32[]{:S(2)}) collective-permute-start(s32[256]{0:T(256)} %get-tuple-element.549), channel_id=1, source_target_pairs={{0,1},{1,2},{2,3},{3,4},{4,5},{5,6},{6,7},{7,8},{8,9},{9,10},{10,1... | collective-permute-start | bytes 3080 | tf_op jit(solution)/shard_map/ppermute | solution.py:33
  37.6 223.5 %collective-permute-start.22 = (s32[256]{0:T(256)}, s32[256]{0:T(256)}, u32[]{:S(2)}, u32[]{:S(2)}) collective-permute-start(s32[256]{0:T(256)} %get-tuple-element.550), channel_id=1, source_target_pairs={{1,0},{2,1},{3,2},{4,3},{5,4},{6,5},{7,6},{8,7},{9,8},{10,9},{11,1... | collective-permute-start | bytes 3080 | tf_op jit(solution)/shard_map/ppermute | solution.py:36
  121.2 79.6 %copy-start.2 = (bf16[2,256,256]{2,1,0:T(8,128)(2,1)S(1)}, bf16[2,256,256]{2,1,0:T(8,128)(2,1)}, u32[]{:S(2)}) copy-start(bf16[2,256,256]{2,1,0:T(8,128)(2,1)} %param.21) | copy-start | bytes 786436
  207.2 46.8 %copy-start.1 = (bf16[2,256,768]{2,1,0:T(8,128)(2,1)S(1)}, bf16[2,256,768]{2,1,0:T(8,128)(2,1)}, u32[]{:S(2)}) copy-start(bf16[2,256,768]{2,1,0:T(8,128)(2,1)} %param.20) | copy-start | bytes 2359300
  208.0 3.1 collective-permute-start.4
  209.4 3.9 collective-permute-start.5
  210.6 4.6 %collective-permute-start.6 = (bf16[128,256]{1,0:T(8,128)(2,1)}, bf16[128,256]{1,0:T(8,128)(2,1)S(1)}, u32[]{:S(2)}, u32[]{:S(2)}) collective-permute-start(bf16[128,256]{1,0:T(8,128)(2,1)} %get-tuple-element.539), channel_id=1, source_target_pairs={{0,3},{1,2},{2,1},{3,0},{4,7},{5,6},{6,5},{7,4},{8,11},{9,10},{10,... | collective-permute-start | bytes 196616 | tf_op jit(solution)/shard_map/ppermute | solution.py:23
  211.1 5.9 %collective-permute-start.7 = (bf16[128,256]{1,0:T(8,128)(2,1)}, bf16[128,256]{1,0:T(8,128)(2,1)S(1)}, u32[]{:S(2)}, u32[]{:S(2)}) collective-permute-start(bf16[128,256]{1,0:T(8,128)(2,1)} %get-tuple-element.538), channel_id=1, source_target_pairs={{0,4},{1,5},{2,6},{3,7},{4,0},{5,1},{6,2},{7,3},{8,12},{9,13},{10,... | collective-permute-start | bytes 196616 | tf_op jit(solution)/shard_map/ppermute | solution.py:23
  213.3 4.7 %collective-permute-start.8 = (bf16[128,256]{1,0:T(8,128)(2,1)}, bf16[128,256]{1,0:T(8,128)(2,1)S(1)}, u32[]{:S(2)}, u32[]{:S(2)}) collective-permute-start(bf16[128,256]{1,0:T(8,128)(2,1)} %get-tuple-element.537), channel_id=1, source_target_pairs={{0,5},{1,4},{2,7},{3,6},{4,1},{5,0},{6,3},{7,2},{8,13},{9,12},{10,... | collective-permute-start | bytes 196616 | tf_op jit(solution)/shard_map/ppermute | solution.py:23
  215.2 5.1 %collective-permute-start.9 = (bf16[128,256]{1,0:T(8,128)(2,1)S(1)}, bf16[128,256]{1,0:T(8,128)(2,1)S(1)}, u32[]{:S(2)}, u32[]{:S(2)}) collective-permute-start(bf16[128,256]{1,0:T(8,128)(2,1)S(1)} %get-tuple-element.536), channel_id=1, source_target_pairs={{0,6},{1,7},{2,4},{3,5},{4,2},{5,3},{6,0},{7,1},{8,14},{9,15},{10,... | collective-permute-start | bytes 196616 | tf_op jit(solution)/shard_map/ppermute | solution.py:23
  216.9 6.1 %collective-permute-start.10 = (bf16[128,256]{1,0:T(8,128)(2,1)S(1)}, bf16[128,256]{1,0:T(8,128)(2,1)S(1)}, u32[]{:S(2)}, u32[]{:S(2)}) collective-permute-start(bf16[128,256]{1,0:T(8,128)(2,1)S(1)} %get-tuple-element.535), channel_id=1, source_target_pairs={{0,7},{1,6},{2,5},{3,4},{4,3},{5,2},{6,1},{7,0},{8,15},{9,14},{10,... | collective-permute-start | bytes 196616 | tf_op jit(solution)/shard_map/ppermute | solution.py:23
  217.9 6.3 %collective-permute-start.11 = (bf16[128,256]{1,0:T(8,128)(2,1)S(1)}, bf16[128,256]{1,0:T(8,128)(2,1)S(1)}, u32[]{:S(2)}, u32[]{:S(2)}) collective-permute-start(bf16[128,256]{1,0:T(8,128)(2,1)S(1)} %get-tuple-element.534), channel_id=1, source_target_pairs={{0,8},{1,9},{2,10},{3,11},{4,12},{5,13},{6,14},{7,15},{8,0},{9,1},... | collective-permute-start | bytes 196616 | tf_op jit(solution)/shard_map/ppermute | solution.py:23
  220.2 9.2 %collective-permute-start.12 = (bf16[128,256]{1,0:T(8,128)(2,1)S(1)}, bf16[128,256]{1,0:T(8,128)(2,1)S(1)}, u32[]{:S(2)}, u32[]{:S(2)}) collective-permute-start(bf16[128,256]{1,0:T(8,128)(2,1)S(1)} %get-tuple-element.533), channel_id=1, source_target_pairs={{0,9},{1,8},{2,11},{3,10},{4,13},{5,12},{6,15},{7,14},{8,1},{9,0},... | collective-permute-start | bytes 196616 | tf_op jit(solution)/shard_map/ppermute | solution.py:23
  223.0 7.5 %collective-permute-start.13 = (bf16[128,256]{1,0:T(8,128)(2,1)S(1)}, bf16[128,256]{1,0:T(8,128)(2,1)S(1)}, u32[]{:S(2)}, u32[]{:S(2)}) collective-permute-start(bf16[128,256]{1,0:T(8,128)(2,1)S(1)} %get-tuple-element.532), channel_id=1, source_target_pairs={{0,10},{1,11},{2,8},{3,9},{4,14},{5,15},{6,12},{7,13},{8,2},{9,3},... | collective-permute-start | bytes 196616 | tf_op jit(solution)/shard_map/ppermute | solution.py:23
  224.3 7.7 %collective-permute-start.14 = (bf16[128,256]{1,0:T(8,128)(2,1)S(1)}, bf16[128,256]{1,0:T(8,128)(2,1)S(1)}, u32[]{:S(2)}, u32[]{:S(2)}) collective-permute-start(bf16[128,256]{1,0:T(8,128)(2,1)S(1)} %get-tuple-element.531), channel_id=1, source_target_pairs={{0,11},{1,10},{2,9},{3,8},{4,15},{5,14},{6,13},{7,12},{8,3},{9,2},... | collective-permute-start | bytes 196616 | tf_op jit(solution)/shard_map/ppermute | solution.py:23
  229.5 6.0 %collective-permute-start.15 = (bf16[128,256]{1,0:T(8,128)(2,1)S(1)}, bf16[128,256]{1,0:T(8,128)(2,1)S(1)}, u32[]{:S(2)}, u32[]{:S(2)}) collective-permute-start(bf16[128,256]{1,0:T(8,128)(2,1)S(1)} %get-tuple-element.530), channel_id=1, source_target_pairs={{0,12},{1,13},{2,14},{3,15},{4,8},{5,9},{6,10},{7,11},{8,4},{9,5},... | collective-permute-start | bytes 196616 | tf_op jit(solution)/shard_map/ppermute | solution.py:23
  230.5 6.4 %collective-permute-start.16 = (bf16[128,256]{1,0:T(8,128)(2,1)S(1)}, bf16[128,256]{1,0:T(8,128)(2,1)S(1)}, u32[]{:S(2)}, u32[]{:S(2)}) collective-permute-start(bf16[128,256]{1,0:T(8,128)(2,1)S(1)} %get-tuple-element.529), channel_id=1, source_target_pairs={{0,13},{1,12},{2,15},{3,14},{4,9},{5,8},{6,11},{7,10},{8,5},{9,4},... | collective-permute-start | bytes 196616 | tf_op jit(solution)/shard_map/ppermute | solution.py:23
  231.9 8.4 %collective-permute-start.17 = (bf16[128,256]{1,0:T(8,128)(2,1)S(1)}, bf16[128,256]{1,0:T(8,128)(2,1)S(1)}, u32[]{:S(2)}, u32[]{:S(2)}) collective-permute-start(bf16[128,256]{1,0:T(8,128)(2,1)S(1)} %get-tuple-element.528), channel_id=1, source_target_pairs={{0,14},{1,15},{2,12},{3,13},{4,10},{5,11},{6,8},{7,9},{8,6},{9,7},... | collective-permute-start | bytes 196616 | tf_op jit(solution)/shard_map/ppermute | solution.py:23
  235.5 9.1 %collective-permute-start.18 = (bf16[128,256]{1,0:T(8,128)(2,1)S(1)}, bf16[128,256]{1,0:T(8,128)(2,1)S(1)}, u32[]{:S(2)}, u32[]{:S(2)}) collective-permute-start(bf16[128,256]{1,0:T(8,128)(2,1)S(1)} %get-tuple-element.527), channel_id=1, source_target_pairs={{0,15},{1,14},{2,13},{3,12},{4,11},{5,10},{6,9},{7,8},{8,7},{9,6},... | collective-permute-start | bytes 196616 | tf_op jit(solution)/shard_map/ppermute | solution.py:23
  240.3 20.8 %copy-start.6 = (s32[1024]{0:T(1024)S(1)}, s32[1024]{0:T(1024)}, u32[]{:S(2)}) copy-start(s32[1024]{0:T(1024)} %copy-done.5) | copy-start | bytes 12292
  255.3 8.5 %collective-permute-start.19 = (bf16[256,512]{1,0:T(8,128)(2,1)}, bf16[256,512]{1,0:T(8,128)(2,1)S(1)}, u32[]{:S(2)}, u32[]{:S(2)}) collective-permute-start(bf16[256,512]{1,0:T(8,128)(2,1)} %get-tuple-element.517), channel_id=1, source_target_pairs={{0,1},{1,2},{2,3},{3,4},{4,5},{5,6},{6,7},{7,8},{8,9},{9,10},{10,1... | collective-permute-start | bytes 786440 | tf_op jit(solution)/shard_map/ppermute | solution.py:33
  259.2 8.8 %collective-permute-start.21 = (bf16[256,512]{1,0:T(8,128)(2,1)}, bf16[256,512]{1,0:T(8,128)(2,1)S(1)}, u32[]{:S(2)}, u32[]{:S(2)}) collective-permute-start(bf16[256,512]{1,0:T(8,128)(2,1)} %get-tuple-element.518), channel_id=1, source_target_pairs={{1,0},{2,1},{3,2},{4,3},{5,4},{6,5},{7,6},{8,7},{9,8},{10,9},{11,1... | collective-permute-start | bytes 786440 | tf_op jit(solution)/shard_map/ppermute | solution.py:36
  345.0 79.1 %copy-start.3 = (bf16[2,256,256]{2,1,0:T(8,128)(2,1)S(1)}, bf16[2,256,256]{2,1,0:T(8,128)(2,1)}, u32[]{:S(2)}) copy-start(bf16[2,256,256]{2,1,0:T(8,128)(2,1)} %param.21) | copy-start | bytes 786436
  (6 other events, 28.6 us)
